TPU v7x, 256 devices: a whole 4x4x8 slice. The times are simulated.
256 devices in a mesh: layer: 32 (over x, y, core), tile: 8 (over z).
Axes of the slice: x: 4, y: 4, z: 8, core: 2. Of those that a mesh axis runs over, the one named last changes fastest.
Arguments:
- down_tiles: bfloat16 [32, 16, 3, 2, 512, 512], P('layer', 'tile'), may hold values from -0.109375 to 0.109375
- up_tiles: bfloat16 [32, 16, 3, 2, 512, 512], P('layer', 'tile'), may hold values from -0.109375 to 0.109375
- down_source: float32 [32, 2, 32, 8192], P('layer', None, None, 'tile'), may hold values from -3 to 3
- up_source: float32 [32, 2, 32, 8192], P('layer', None, None, 'tile'), may hold values from -3 to 3
- thickness: int32 [32], P('layer'), may hold values from 1 to 2
Outputs:
- field: float32 [32, 2, 32, 8192], P('layer', None, None, 'tile')
All inputs are finite; a program needn't handle non-finite values.
Results may differ from a plain program's by a relative error of at most 0.04.
Values may be sent and summed in bfloat16 or wider, within the bound.
No kernel may reach another device: no remote copies, remote signals or barrier semaphores. Data moves between devices by JAX's collectives and lax.ppermute only.
A program may use at most 64 MiB of HBM per device.

v0:
```python
import functools

import jax
import jax.numpy as jnp
from jax import lax
from jax.experimental import pallas as pl
from jax.experimental.pallas import tpu as pltpu
from jax.sharding import PartitionSpec as P

AXES = ("layer", "tile")


VMEM = pl.BlockSpec(memory_space=pltpu.VMEM)
HBM = pl.BlockSpec(memory_space=pltpu.HBM)
SMEM = pl.BlockSpec(memory_space=pltpu.SMEM)


def pick_kernel(info, down, up, out, held, into, back):
    row, upward = info[0], info[1]

    for index, source in enumerate((down, up)):

        @pl.when(upward == index)
        def _(source=source):
            for k in range(3):
                pltpu.make_async_copy(source.at[0, row, k], held.at[k], into.at[k]).start()

    for k in range(3):
        pltpu.make_async_copy(down.at[0, 0, k], held.at[k], into.at[k]).wait()
        pltpu.make_async_copy(held.at[k], out.at[k], back.at[k]).start()
    for k in range(3):
        pltpu.make_async_copy(held.at[k], out.at[k], back.at[k]).wait()


def pick_row(info, down, up):
    return pl.pallas_call(
        pick_kernel,
        out_shape=jax.ShapeDtypeStruct((4,) + down.shape[3:], down.dtype),
        in_specs=[SMEM, HBM, HBM],
        out_specs=HBM,
        scratch_shapes=[
            pltpu.VMEM((3,) + down.shape[3:], down.dtype),
            pltpu.SemaphoreType.DMA((3,)),
            pltpu.SemaphoreType.DMA((3,)),
        ],
        compiler_params=pltpu.CompilerParams(vmem_limit_bytes=8 << 20),
        name="pick_row",
    )(info, down, up)


def begin_kernel(count, info, *refs):
    inputs, (down, up, other, later) = refs[:count], refs[count : count + 4]
    partial, left, held, sems = refs[count + 4 :]
    slot, row, near_k, far_k = info[0], info[1], info[2], info[3]
    places = [held.at[n] for n in range(count)] + [left.at[n] for n in range(3 - count)]

    for index, source in enumerate((down.at[0, row], up.at[0, row], other, later)):

        @pl.when(slot == index)
        def _(source=source):
            for n, k in enumerate((1, near_k, far_k)):
                pltpu.make_async_copy(source.at[k], places[n], sems.at[n]).start()

    for n in range(count):
        pltpu.make_async_copy(other.at[n], places[n], sems.at[n]).wait()
        for part in range(2):
            value = jnp.dot(inputs[n][...], held[n, part], preferred_element_type=jnp.float32)
            partial[part] = value if n == 0 else partial[part] + value
    for n in range(count, 3):
        pltpu.make_async_copy(other.at[n], places[n], sems.at[n]).wait()


def begin_apply(info, inputs, tiles):
    rows, width = inputs[0].shape
    count = len(inputs)
    return pl.pallas_call(
        functools.partial(begin_kernel, count),
        out_shape=(
            jax.ShapeDtypeStruct((2, rows, width), jnp.float32),
            jax.ShapeDtypeStruct((3 - count, 2, width, width), jnp.bfloat16),
        ),
        in_specs=[SMEM] + [VMEM] * count + [HBM] * 4,
        out_specs=(VMEM, VMEM),
        scratch_shapes=[
            pltpu.VMEM((count, 2, width, width), jnp.bfloat16),
            pltpu.SemaphoreType.DMA((3,)),
        ],
        compiler_params=pltpu.CompilerParams(vmem_limit_bytes=8 << 20),
        cost_estimate=pl.CostEstimate(
            flops=4 * count * rows * width * width,
            bytes_accessed=12 * width * width,
            transcendentals=0,
        ),
        name="begin_apply",
    )(info, *inputs, *tiles)


def end_kernel(count, *refs):
    inputs, (partial, left, source, new, value) = refs[:count], refs[count:]
    columns = source.shape[0] // 2
    totals = []
    for part in range(2):
        total = partial[part]
        for n in range(count):
            total += jnp.dot(inputs[n][...], left[n, part], preferred_element_type=jnp.float32)
        totals.append(total)
    real, imag = totals
    for half, result in enumerate(
        (real[:columns] - imag[columns:], real[columns:] + imag[:columns])
    ):
        rows = pl.ds(half * columns, columns)
        result = result + source[rows]
        value[rows] = result
        new[rows] = result.astype(new.dtype)


def end_apply(inputs, partial, left, source):
    rows, width = source.shape
    count = len(inputs)
    return pl.pallas_call(
        functools.partial(end_kernel, count),
        out_shape=(
            jax.ShapeDtypeStruct((rows, width), jnp.bfloat16),
            jax.ShapeDtypeStruct((rows, width), jnp.float32),
        ),
        in_specs=[VMEM] * (count + 3),
        out_specs=(VMEM, VMEM),
        compiler_params=pltpu.CompilerParams(vmem_limit_bytes=8 << 20),
        cost_estimate=pl.CostEstimate(
            flops=4 * count * rows * width * width,
            bytes_accessed=8 * rows * width,
            transcendentals=0,
        ),
        name="end_apply",
    )(*inputs, partial, left, source)


def shards(down_tiles, up_tiles, down_source, up_source, thickness):
    layers, tile_count = lax.axis_size("layer"), lax.axis_size("tile")
    chips = layers // 2
    layer, tile = lax.axis_index("layer"), lax.axis_index("tile")
    chip, core = layer // 2, layer % 2
    half = tile_count // 2
    edge = jnp.where(tile < half, core, 1 - core)
    width = down_tiles.shape[-1]
    columns = down_source.shape[2]

    def at(chip_index, core_index, tile_index):
        return (2 * chip_index + core_index) * tile_count + tile_index

    def swaps(pairs):
        return [pair for a, b in pairs for pair in ((a, b), (b, a))]

    inside = swaps((at(i, 0, z), at(i, 1, z)) for i in range(chips) for z in range(tile_count))
    def side(c, z):
        return c if z < half else 1 - c

    def beyond(c, z):
        target = z + 1 if side(c, z) else z - 1
        if not 0 <= target < tile_count:
            return None
        return next(d for d in range(2) if side(d, target) != side(c, z)), target

    along = swaps(
        (at(i, c, z), at(i, *beyond(c, z)))
        for i in range(chips)
        for z in range(tile_count - 1)
        for c in range(2)
        if side(c, z)
    )
    hops = [
        swaps(
            (at(i, c, z), at(i + 1, c, z))
            for i in range(start, chips - 1, 2)
            for c in range(2)
            for z in range(tile_count)
        )
        for start in range(2)
    ]

    corners = [
        swaps(
            (at(i, c, z), at(i + 1, *beyond(c, z)))
            for i in range(start, chips - 1, 2)
            for c in range(2)
            for z in range(tile_count)
            if beyond(c, z)
        )
        for start in range(2)
    ]

    def piece(source, which):
        cut = lax.dynamic_slice_in_dim(source[0], which * width, width, axis=2)
        return cut.reshape(1, 2 * columns, width)

    firstly = (chip >= chips // 2).astype(jnp.int32)
    picks = [
        pick_row(jnp.stack([1 - edge, which]), down_tiles, up_tiles)
        for which in (firstly, 1 - firstly)
    ]
    early_tiles = lax.ppermute(picks[0], AXES, inside)
    sent_source = jnp.concatenate([piece(down_source, 1 - edge), piece(up_source, 1 - edge)])
    other_source = lax.ppermute(sent_source, AXES, inside)
    other_thick = lax.ppermute(thickness, AXES, inside)
    picked, early_tiles, other_source, other_thick = lax.optimization_barrier(
        (picks[1], early_tiles, other_source, other_thick)
    )
    others = (early_tiles, lax.ppermute(picked, AXES, inside))
    sums = jnp.concatenate([piece(down_source, edge), piece(up_source, edge), other_source])
    own_thick, other_thick = thickness[0], other_thick[0]
    low_thick = jnp.where(core == 0, own_thick, other_thick)
    high_thick = jnp.where(core == 0, other_thick, own_thick)
    near_k, far_k = 2 - 2 * edge, 2 * edge

    def slot_of(upward, place):
        position = jnp.where(upward, 1 - place, place)
        return upward.astype(jnp.int32) + 2 * (position != core).astype(jnp.int32)

    def apply(step, index, trace, far, sums, kept_if, others):
        upward = (step < chips // 2) != (chip < chips // 2)
        first = jnp.where(upward, high_thick, low_thick)
        place = (index >= first).astype(jnp.int32)
        last = kept_if & ((index == first - 1) | (index == low_thick + high_thick - 1))
        slot = slot_of(upward, place)
        second = jnp.asarray(step >= chips // 2).astype(jnp.int32)
        info = jnp.stack([jnp.where(slot < 2, slot, 2 + second), edge, near_k, far_k])
        if far is None:
            far = lax.ppermute(trace, AXES, along)
            near = lax.ppermute(trace, AXES, inside)
            early, late = [trace, near], [far]
        else:
            near = lax.ppermute(trace, AXES, inside)
            early, late = [trace], [near, far]
        partial, left = begin_apply(info, early, (down_tiles, up_tiles, *others))
        held = lax.dynamic_index_in_dim(sums, slot, 0, False)
        new, value = end_apply(late, partial, left, jnp.where(last, held, 0))
        kept = jnp.where(last, value, held)
        return new, lax.dynamic_update_index_in_dim(sums, kept, slot, 0)

    def one_step(step, state):
        upward = (step < chips // 2) != (chip < chips // 2)
        live = (chip == step) | (chip == chips - 1 - step)
        sending = (chip == step - 1) | (chip == chips - step)
        taking = ((chip == step) & (chip > 0)) | (
            (chip == chips - 1 - step) & (chip < chips - 1)
        )
        parity = (step + 1) % 2
        first = jnp.where(upward, high_thick, low_thick)
        count = low_thick + high_thick

        def hop(start):
            def move(trace, sums):
                moved = lax.ppermute(trace, AXES, hops[start])
                corner = lax.ppermute(trace, AXES, corners[start])
                return apply(step, 0, moved, corner, sums, taking, others)

            return move

        state = lax.switch(
            jnp.where(sending | taking, 1 + parity, 0),
            [lambda trace, sums: (trace, sums), hop(0), hop(1)],
            *state,
        )
        begin = jnp.where(taking, 1, first)
        end = jnp.where(live, count, begin)
        return lax.fori_loop(
            begin, end, lambda index, s: apply(step, index, s[0], None, s[1], live, others), state
        )

    begin_slot = slot_of(chip >= chips // 2, 0)
    trace = lax.dynamic_index_in_dim(sums, begin_slot, 0, False).astype(jnp.bfloat16)
    starting = (chip == 0) | (chip == chips - 1)
    begin = jnp.where(chip < chips // 2, low_thick, high_thick)
    state = lax.fori_loop(
        begin,
        jnp.where(starting, low_thick + high_thick, begin),
        lambda index, s: apply(0, index, s[0], None, s[1], starting, (others[0], others[0])),
        (trace, sums),
    )
    _, sums = lax.fori_loop(1, chips, one_step, state)
    own_field = sums[0] + sums[1]
    other_field = lax.ppermute(sums[2] + sums[3], AXES, inside)
    left = jnp.where(edge == 0, own_field, other_field)
    right = jnp.where(edge == 0, other_field, own_field)
    return jnp.concatenate([left, right], axis=1).reshape(1, 2, columns, 2 * width)


def solution(mesh):
    return jax.shard_map(
        shards,
        mesh=mesh,
        in_specs=(
            P("layer", "tile", None, None, None, None),
            P("layer", "tile", None, None, None, None),
            P("layer", None, None, "tile"),
            P("layer", None, None, "tile"),
            P("layer"),
        ),
        out_specs=P("layer", None, None, "tile"),
        check_vma=False,
    )
```

profile of v0, /device:TPU:1, one launch (start us, length us, event | category | flops | bytes accessed | tf_op | source)
XLA Modules:
  0.0 357.6 jit_solution(9648017618559017206)
XLA Ops:
  0.1 3.5 pick_row.3
  3.6 3.3 collective-permute-start.10
  6.9 0.1 collective-permute-start.11
  7.1 0.5 collective-permute-start.12
  7.6 3.5 pick_row.2
  11.1 3.3 collective-permute-done.12
  14.4 0.4 collective-permute-start.13
  16.7 7.9 %while.71 = (s32[]{:T(128)}, bf16[64,512]{1,0:T(8,128)(2,1)S(1)}, f32[4,64,512]{2,1,0:T(8,128)S(1)}, s32[]{:T(128)}, pred[]{:T(512)}, /*index=5*/s32[]{:T(128)},...) while((s32[]{:T(128)}, bf16[64,512]{1,0:T(8,128)(2,1)S(1)}, ...), condition=%wide.region_1.2_spmd, body=%wide.region_0.1_spmd.sunk | while | flops 201392144 | bytes 4850129 | solution.py:274
  16.8 0.2 collective-permute-start.7
  17.0 2.1 collective-permute-start.6
  19.3 2.6 collective-permute-done.7.refs_1_
  21.9 2.4 begin_apply.12
  24.3 0.3 end_apply.12
  24.7 330.7 %while.73 = (s32[]{:T(128)}, bf16[64,512]{1,0:T(8,128)(2,1)S(1)}, f32[4,64,512]{2,1,0:T(8,128)S(1)}, s32[]{:T(128)}, pred[]{:T(512)}, /*index=5*/pred[]{:T(512)}...) while((s32[]{:T(128)}, bf16[64,512]{1,0:T(8,128)(2,1)S(1)}, ...), condition=%wide.region_8.9_spmd, body=%wide.region_2.8_spmd.sunk | while | flops 402784352 | bytes 9963307 | solution.py:280
  24.7 7.8 %conditional.2 = ((bf16[64,512]{1,0:T(8,128)(2,1)S(1)}, f32[4,64,512]{2,1,0:T(8,128)S(1)})) conditional(s32[]{:T(128)} %clamp.17, (bf16[64,512]{1,0:T(8,128)(2,1)S(1)}, f32[4,64,512]{2,1,0:T(8,128)S(1)}) %tuple.125, (bf16[64,512]{1,0:T(8,128)(2,1)S(1)}, s32[]{:T(128)}, s32[]{:T(128)}, s32[]{:T(128)}, s32[]{:T(128)}, ...), branch_computations={%region_3.3_spmd, %region_4.4_spmd, %region_5.5_spmd} | conditional | flops 201392160 | bytes 5112252 | solution.py:259
  24.8 0.1 collective-permute-start
  24.9 3.5 collective-permute-start.2
  28.5 1.0 collective-permute-start.1
  29.6 2.4 begin_apply.10
  32.0 0.5 end_apply.10
  34.4 313.7 %conditional.2 = ((bf16[64,512]{1,0:T(8,128)(2,1)S(1)}, f32[4,64,512]{2,1,0:T(8,128)S(1)})) conditional(s32[]{:T(128)} %clamp.17, (bf16[64,512]{1,0:T(8,128)(2,1)S(1)}, f32[4,64,512]{2,1,0:T(8,128)S(1)}) %tuple.125, (bf16[64,512]{1,0:T(8,128)(2,1)S(1)}, s32[]{:T(128)}, s32[]{:T(128)}, s32[]{:T(128)}, s32[]{:T(128)}, ...), branch_computations={%region_3.3_spmd, %region_4.4_spmd, %region_5.5_spmd} | conditional | flops 201392160 | bytes 5112252 | solution.py:259
  34.5 306.7 %collective-permute-start = (bf16[64,512]{1,0:T(8,128)(2,1)S(1)}, bf16[64,512]{1,0:T(8,128)(2,1)S(1)}, u32[]{:S(2)}, u32[]{:S(2)}) collective-permute-start(bf16[64,512]{1,0:T(8,128)(2,1)S(1)} %get-tuple-element.1233), channel_id=1, source_target_pairs={{0,16},{16,0},{1,17},{17,1},{2,18},{18,2},{3,19},{19,3},{4,20},{20... | collective-permute-start | bytes 196616 | tf_op jit(solution)/shard_map/while/body/eval_jaxpr/cond/branch_1_fun/ppermute | solution.py:253
  341.1 2.7 collective-permute-start.2
  344.1 2.4 begin_apply.10
  346.5 1.1 collective-permute-done.2.refs_1_
  347.6 0.5 end_apply.10
  348.2 7.2 %while.74 = (s32[]{:T(128)}, bf16[64,512]{1,0:T(8,128)(2,1)S(1)}, f32[4,64,512]{2,1,0:T(8,128)S(1)}, s32[]{:T(128)}, pred[]{:T(512)}, /*index=5*/s32[]{:T(128)},...) while((s32[]{:T(128)}, bf16[64,512]{1,0:T(8,128)(2,1)S(1)}, ...), condition=%wide.region_7.7_spmd, body=%wide.region_6.6_spmd.sunk | while | flops 201392160 | bytes 4850162 | solution.py:266
  348.3 4.1 %collective-permute-start.8 = (bf16[64,512]{1,0:T(8,128)(2,1)S(1)}, bf16[64,512]{1,0:T(8,128)(2,1)S(1)}, u32[]{:S(2)}, u32[]{:S(2)}) collective-permute-start(bf16[64,512]{1,0:T(8,128)(2,1)S(1)} %get-tuple-element.1859.refs_0_), channel_id=1, source_target_pairs={{8,1},{1,8},{9,2},{2,9},{10,3},{3,10},{11,12},{12,11},{4,13},{13,4... | collective-permute-start | bytes 196616 | tf_op jit(solution)/shard_map/while/body/eval_jaxpr/while/body/ppermute | solution.py:228
  352.6 2.4 begin_apply.13
  355.0 0.3 end_apply.13
  355.5 1.3 collective-permute-done.14
  356.9 0.7 pad_maximum_fusion.2
  (69 shorter events, 1.5 us)
Async XLA Ops:
  0.1 6.8 %copy-start = (f32[1,2,32,1024]{3,2,1,0:T(8,128)S(1)}, f32[1,2,32,1024]{3,2,1,0:T(8,128)}, u32[]{:S(2)}) copy-start(f32[1,2,32,1024]{3,2,1,0:T(8,128)} %param.17) | copy-start | bytes 786436
  0.1 6.8 %copy-start.1 = (f32[1,2,32,1024]{3,2,1,0:T(8,128)S(1)}, f32[1,2,32,1024]{3,2,1,0:T(8,128)}, u32[]{:S(2)}) copy-start(f32[1,2,32,1024]{3,2,1,0:T(8,128)} %param.16) | copy-start | bytes 786436
  3.6 10.8 %collective-permute-start.10 = (bf16[4,2,512,512]{3,2,1,0:T(8,128)(2,1)}, bf16[4,2,512,512]{3,2,1,0:T(8,128)(2,1)}, u32[]{:S(2)}, u32[]{:S(2)}) collective-permute-start(bf16[4,2,512,512]{3,2,1,0:T(8,128)(2,1)} %pick_row.3), channel_id=1, source_target_pairs={{0,8},{8,0},{1,9},{9,1},{2,10},{10,2},{3,11},{11,3},{4,12},{12,4},... | collective-permute-start | bytes 12582920 | tf_op jit(solution)/shard_map/ppermute | solution.py:201
  6.9 7.4 %collective-permute-start.11 = (f32[2,64,512]{2,1,0:T(8,128)S(1)}, f32[2,64,512]{2,1,0:T(8,128)S(1)}, u32[]{:S(2)}, u32[]{:S(2)}) collective-permute-start(f32[2,64,512]{2,1,0:T(8,128)S(1)} %pad_maximum_fusion.1), channel_id=1, source_target_pairs={{0,8},{8,0},{1,9},{9,1},{2,10},{10,2},{3,11},{11,3},{4,12},{12,4},... | collective-permute-start | bytes 786440 | tf_op jit(solution)/shard_map/ppermute | solution.py:203
  7.1 7.3 %collective-permute-start.12 = (s32[1]{0:T(128)}, s32[1]{0:T(128)}, u32[]{:S(2)}, u32[]{:S(2)}) collective-permute-start(s32[1]{0:T(128)} %param.18), channel_id=1, source_target_pairs={{0,8},{8,0},{1,9},{9,1},{2,10},{10,2},{3,11},{11,3},{4,12},{12,4},... | collective-permute-start | bytes 20 | tf_op jit(solution)/shard_map/ppermute | solution.py:204
  14.4 10.3 %collective-permute-start.13 = (bf16[4,2,512,512]{3,2,1,0:T(8,128)(2,1)}, bf16[4,2,512,512]{3,2,1,0:T(8,128)(2,1)}, u32[]{:S(2)}, u32[]{:S(2)}) collective-permute-start(bf16[4,2,512,512]{3,2,1,0:T(8,128)(2,1)} %pick_row.2), channel_id=1, source_target_pairs={{0,8},{8,0},{1,9},{9,1},{2,10},{10,2},{3,11},{11,3},{4,12},{12,4},... | collective-permute-start | bytes 12582920 | tf_op jit(solution)/shard_map/ppermute | solution.py:208
  16.8 5.1 %collective-permute-start.7 = (bf16[64,512]{1,0:T(8,128)(2,1)S(1)}, bf16[64,512]{1,0:T(8,128)(2,1)S(1)}, u32[]{:S(2)}, u32[]{:S(2)}) collective-permute-start(bf16[64,512]{1,0:T(8,128)(2,1)S(1)} %get-tuple-element.1923.refs_0_), channel_id=1, source_target_pairs={{0,8},{8,0},{1,9},{9,1},{2,10},{10,2},{3,11},{11,3},{4,12},{12,4},... | collective-permute-start | bytes 196616 | tf_op jit(solution)/shard_map/while/body/ppermute | solution.py:229
  17.0 7.3 %collective-permute-start.6 = (bf16[64,512]{1,0:T(8,128)(2,1)S(1)}, bf16[64,512]{1,0:T(8,128)(2,1)S(1)}, u32[]{:S(2)}, u32[]{:S(2)}) collective-permute-start(bf16[64,512]{1,0:T(8,128)(2,1)S(1)} %get-tuple-element.1923.refs_0_), channel_id=1, source_target_pairs={{8,1},{1,8},{9,2},{2,9},{10,3},{3,10},{11,12},{12,11},{4,13},{13,4... | collective-permute-start | bytes 196616 | tf_op jit(solution)/shard_map/while/body/ppermute | solution.py:228
  24.8 3.7 %collective-permute-start = (bf16[64,512]{1,0:T(8,128)(2,1)S(1)}, bf16[64,512]{1,0:T(8,128)(2,1)S(1)}, u32[]{:S(2)}, u32[]{:S(2)}) collective-permute-start(bf16[64,512]{1,0:T(8,128)(2,1)S(1)} %get-tuple-element.1233), channel_id=1, source_target_pairs={{0,16},{16,0},{1,17},{17,1},{2,18},{18,2},{3,19},{19,3},{4,20},{20... | collective-permute-start | bytes 196616 | tf_op jit(solution)/shard_map/while/body/eval_jaxpr/cond/branch_1_fun/ppermute | solution.py:253
  24.9 7.2 %collective-permute-start.2 = (bf16[64,512]{1,0:T(8,128)(2,1)S(1)}, bf16[64,512]{1,0:T(8,128)(2,1)S(1)}, u32[]{:S(2)}, u32[]{:S(2)}) collective-permute-start(bf16[64,512]{1,0:T(8,128)(2,1)S(1)} %get-tuple-element.1233), channel_id=1, source_target_pairs={{1,24},{24,1},{2,25},{25,2},{3,26},{26,3},{4,29},{29,4},{5,30},{30... | collective-permute-start | bytes 196616 | tf_op jit(solution)/shard_map/while/body/eval_jaxpr/cond/branch_1_fun/ppermute | solution.py:254
  28.5 3.5 collective-permute-start.1
  34.5 309.5 %collective-permute-start = (bf16[64,512]{1,0:T(8,128)(2,1)S(1)}, bf16[64,512]{1,0:T(8,128)(2,1)S(1)}, u32[]{:S(2)}, u32[]{:S(2)}) collective-permute-start(bf16[64,512]{1,0:T(8,128)(2,1)S(1)} %get-tuple-element.1233), channel_id=1, source_target_pairs={{0,16},{16,0},{1,17},{17,1},{2,18},{18,2},{3,19},{19,3},{4,20},{20... | collective-permute-start | bytes 196616 | tf_op jit(solution)/shard_map/while/body/eval_jaxpr/cond/branch_1_fun/ppermute | solution.py:253
  341.1 6.5 %collective-permute-start.2 = (bf16[64,512]{1,0:T(8,128)(2,1)S(1)}, bf16[64,512]{1,0:T(8,128)(2,1)S(1)}, u32[]{:S(2)}, u32[]{:S(2)}) collective-permute-start(bf16[64,512]{1,0:T(8,128)(2,1)S(1)} %get-tuple-element.1233), channel_id=1, source_target_pairs={{1,24},{24,1},{2,25},{25,2},{3,26},{26,3},{4,29},{29,4},{5,30},{30... | collective-permute-start | bytes 196616 | tf_op jit(solution)/shard_map/while/body/eval_jaxpr/cond/branch_1_fun/ppermute | solution.py:254
  343.9 3.7 %collective-permute-start.1 = (bf16[64,512]{1,0:T(8,128)(2,1)S(1)}, bf16[64,512]{1,0:T(8,128)(2,1)S(1)}, u32[]{:S(2)}, u32[]{:S(2)}) collective-permute-start(bf16[64,512]{1,0:T(8,128)(2,1)S(1)} %collective-permute-done.refs_0_), channel_id=1, source_target_pairs={{0,8},{8,0},{1,9},{9,1},{2,10},{10,2},{3,11},{11,3},{4,12},{12,4},... | collective-permute-start | bytes 196616 | tf_op jit(solution)/shard_map/while/body/eval_jaxpr/cond/branch_1_fun/ppermute | solution.py:232
  348.2 4.4 %collective-permute-start.9 = (bf16[64,512]{1,0:T(8,128)(2,1)S(1)}, bf16[64,512]{1,0:T(8,128)(2,1)S(1)}, u32[]{:S(2)}, u32[]{:S(2)}) collective-permute-start(bf16[64,512]{1,0:T(8,128)(2,1)S(1)} %get-tuple-element.1859.refs_0_), channel_id=1, source_target_pairs={{0,8},{8,0},{1,9},{9,1},{2,10},{10,2},{3,11},{11,3},{4,12},{12,4},... | collective-permute-start | bytes 196616 | tf_op jit(solution)/shard_map/while/body/eval_jaxpr/while/body/ppermute | solution.py:229
  348.3 6.7 %collective-permute-start.8 = (bf16[64,512]{1,0:T(8,128)(2,1)S(1)}, bf16[64,512]{1,0:T(8,128)(2,1)S(1)}, u32[]{:S(2)}, u32[]{:S(2)}) collective-permute-start(bf16[64,512]{1,0:T(8,128)(2,1)S(1)} %get-tuple-element.1859.refs_0_), channel_id=1, source_target_pairs={{8,1},{1,8},{9,2},{2,9},{10,3},{3,10},{11,12},{12,11},{4,13},{13,4... | collective-permute-start | bytes 196616 | tf_op jit(solution)/shard_map/while/body/eval_jaxpr/while/body/ppermute | solution.py:228
  355.4 1.4 collective-permute-start.14
where the time goes:
time: 365 us; the launch traced here: 358 us
  starting transfers between devices  325 us (89%)
  Pallas kernels  18.3 us (5%)
  waiting for transfers between devices  8.3 us (2%)
    ppermute x2, starting transfers between devices, move(): moved = lax.ppermute(trace, AXES, hops[start])  307 us
    pallas_call x4, Pallas kernels, begin_apply(): pl.pallas_call(functools.partial(begin_kernel, count), out_shape=(jax.Sha...  9.72 us
  transfers between devices with their start and end apart: 15, of which 4 were waited for; matrix products, arithmetic and copies ran while one was open for 0% of the time, Pallas kernels for 4%

commit v1 on v0

--- a/solution.py
+++ b/solution.py
@@ -32,10 +32,10 @@
         pltpu.make_async_copy(held.at[k], out.at[k], back.at[k]).wait()
 
 
-def pick_row(info, down, up):
+def pick_row(info, down, up, rows):
     return pl.pallas_call(
         pick_kernel,
-        out_shape=jax.ShapeDtypeStruct((4,) + down.shape[3:], down.dtype),
+        out_shape=jax.ShapeDtypeStruct((rows,) + down.shape[3:], down.dtype),
         in_specs=[SMEM, HBM, HBM],
         out_specs=HBM,
         scratch_shapes=[
@@ -195,8 +195,8 @@
 
     firstly = (chip >= chips // 2).astype(jnp.int32)
     picks = [
-        pick_row(jnp.stack([1 - edge, which]), down_tiles, up_tiles)
-        for which in (firstly, 1 - firstly)
+        pick_row(jnp.stack([1 - edge, which]), down_tiles, up_tiles, rows)
+        for which, rows in ((firstly, 3), (1 - firstly, 4))
     ]
     early_tiles = lax.ppermute(picks[0], AXES, inside)
     sent_source = jnp.concatenate([piece(down_source, 1 - edge), piece(up_source, 1 - edge)])

time: 365 us -> 396 us (1.085)
  starting transfers between devices: 325 us -> 355 us
    ppermute x2, starting transfers between devices: 307 us -> 333 us  [move(): moved = lax.ppermute(trace, AXES, hops[start])]
    ppermute x2 -> x3, starting transfers between devices: 6.16 us -> 9.7 us  [apply(): far = lax.ppermute(trace, AXES, along)]
    pallas_call x4 -> x5, Pallas kernels: 9.72 us -> 12.2 us  [begin_apply(): pl.pallas_call(functools.partial(begin_kernel, count), out_shape=(jax.Sha...]
  transfers between devices with their start and end apart: 15 -> 17, of which waited for: 4 -> 4; matrix products, arithmetic and copies ran while one was open for 0% -> 1% of each run, Pallas kernels for 4% -> 4%
where the time goes in v1:
time: 396 us; the launch traced here: 389 us
  starting transfers between devices  355 us (90%)
  Pallas kernels  20 us (5%)
  waiting for transfers between devices  4.5 us (1%)
    ppermute x2, starting transfers between devices, move(): moved = lax.ppermute(trace, AXES, hops[start])  333 us
    pallas_call x5, Pallas kernels, begin_apply(): pl.pallas_call(functools.partial(begin_kernel, count), out_shape=(jax.Sha...  12.2 us
    ppermute x3, starting transfers between devices, apply(): far = lax.ppermute(trace, AXES, along)  9.7 us
  transfers between devices with their start and end apart: 17, of which 4 were waited for; matrix products, arithmetic and copies ran while one was open for 1% of the time, Pallas kernels for 4%

profile of v1, /device:TPU:1, one launch (start us, length us, event | category | flops | bytes accessed | tf_op | source)
XLA Modules:
  0.0 388.6 jit_solution(1038031665505463486)
XLA Ops:
  0.1 2.5 pick_row.3
  2.6 3.3 collective-permute-start.10
  5.9 1.1 constant_dynamic-slice_fusion.4
  7.0 0.7 pad_maximum_fusion.1
  7.8 0.5 collective-permute-start.12
  8.4 3.5 pick_row.2
  13.9 1.0 pad_maximum_fusion
  14.9 7.4 %while.71 = (s32[]{:T(128)}, bf16[64,512]{1,0:T(8,128)(2,1)S(1)}, f32[4,64,512]{2,1,0:T(8,128)S(1)}, s32[]{:T(128)}, pred[]{:T(512)}, /*index=5*/s32[]{:T(128)},...) while((s32[]{:T(128)}, bf16[64,512]{1,0:T(8,128)(2,1)S(1)}, ...), condition=%wide.region_1.2_spmd, body=%wide.region_0.1_spmd.sunk | while | flops 201392144 | bytes 4850129 | solution.py:274
  14.9 0.5 collective-permute-start.7
  15.4 1.9 collective-permute-start.6
  17.5 2.0 collective-permute-done.7.refs_1_
  19.5 2.4 begin_apply.12
  21.9 0.3 end_apply.12
  22.3 364.1 %while.73 = (s32[]{:T(128)}, bf16[64,512]{1,0:T(8,128)(2,1)S(1)}, f32[4,64,512]{2,1,0:T(8,128)S(1)}, s32[]{:T(128)}, pred[]{:T(512)}, /*index=5*/pred[]{:T(512)}...) while((s32[]{:T(128)}, bf16[64,512]{1,0:T(8,128)(2,1)S(1)}, ...), condition=%wide.region_8.9_spmd, body=%wide.region_2.8_spmd.sunk | while | flops 402784352 | bytes 9963307 | solution.py:280
  22.3 7.7 %conditional.2 = ((bf16[64,512]{1,0:T(8,128)(2,1)S(1)}, f32[4,64,512]{2,1,0:T(8,128)S(1)})) conditional(s32[]{:T(128)} %clamp.17, (bf16[64,512]{1,0:T(8,128)(2,1)S(1)}, f32[4,64,512]{2,1,0:T(8,128)S(1)}) %tuple.125, (bf16[64,512]{1,0:T(8,128)(2,1)S(1)}, s32[]{:T(128)}, s32[]{:T(128)}, s32[]{:T(128)}, s32[]{:T(128)}, ...), branch_computations={%region_3.3_spmd, %region_4.4_spmd, %region_5.5_spmd} | conditional | flops 201392160 | bytes 5112252 | solution.py:259
  22.5 3.3 collective-permute-start.2
  26.0 1.0 collective-permute-start.1
  27.0 2.4 begin_apply.10
  29.5 0.5 end_apply.10
  31.9 340.4 %conditional.2 = ((bf16[64,512]{1,0:T(8,128)(2,1)S(1)}, f32[4,64,512]{2,1,0:T(8,128)S(1)})) conditional(s32[]{:T(128)} %clamp.17, (bf16[64,512]{1,0:T(8,128)(2,1)S(1)}, f32[4,64,512]{2,1,0:T(8,128)S(1)}) %tuple.125, (bf16[64,512]{1,0:T(8,128)(2,1)S(1)}, s32[]{:T(128)}, s32[]{:T(128)}, s32[]{:T(128)}, s32[]{:T(128)}, ...), branch_computations={%region_3.3_spmd, %region_4.4_spmd, %region_5.5_spmd} | conditional | flops 201392160 | bytes 5112252 | solution.py:259
  31.9 333.4 %collective-permute-start = (bf16[64,512]{1,0:T(8,128)(2,1)S(1)}, bf16[64,512]{1,0:T(8,128)(2,1)S(1)}, u32[]{:S(2)}, u32[]{:S(2)}) collective-permute-start(bf16[64,512]{1,0:T(8,128)(2,1)S(1)} %get-tuple-element.1233), channel_id=1, source_target_pairs={{0,16},{16,0},{1,17},{17,1},{2,18},{18,2},{3,19},{19,3},{4,20},{20... | collective-permute-start | bytes 196616 | tf_op jit(solution)/shard_map/while/body/eval_jaxpr/cond/branch_1_fun/ppermute | solution.py:253
  365.3 2.7 collective-permute-start.2
  368.3 2.4 begin_apply.10
  370.7 1.1 collective-permute-done.2.refs_1_
  371.8 0.5 end_apply.10
  372.4 14.0 %while.74 = (s32[]{:T(128)}, bf16[64,512]{1,0:T(8,128)(2,1)S(1)}, f32[4,64,512]{2,1,0:T(8,128)S(1)}, s32[]{:T(128)}, pred[]{:T(512)}, /*index=5*/s32[]{:T(128)},...) while((s32[]{:T(128)}, bf16[64,512]{1,0:T(8,128)(2,1)S(1)}, ...), condition=%wide.region_7.7_spmd, body=%wide.region_6.6_spmd.sunk | while | flops 201392160 | bytes 4850162 | solution.py:266
  372.5 4.1 %collective-permute-start.8 = (bf16[64,512]{1,0:T(8,128)(2,1)S(1)}, bf16[64,512]{1,0:T(8,128)(2,1)S(1)}, u32[]{:S(2)}, u32[]{:S(2)}) collective-permute-start(bf16[64,512]{1,0:T(8,128)(2,1)S(1)} %get-tuple-element.1859.refs_0_), channel_id=1, source_target_pairs={{8,1},{1,8},{9,2},{2,9},{10,3},{3,10},{11,12},{12,11},{4,13},{13,4... | collective-permute-start | bytes 196616 | tf_op jit(solution)/shard_map/while/body/eval_jaxpr/while/body/ppermute | solution.py:228
  376.8 2.4 begin_apply.13
  379.7 3.7 collective-permute-start.8
  383.6 2.4 begin_apply.13
  386.5 1.3 collective-permute-done.14
  387.9 0.7 pad_maximum_fusion.2
  (75 shorter events, 2.7 us)
Async XLA Ops:
  2.6 9.3 %collective-permute-start.10 = (bf16[3,2,512,512]{3,2,1,0:T(8,128)(2,1)S(1)}, bf16[3,2,512,512]{3,2,1,0:T(8,128)(2,1)}, u32[]{:S(2)}, u32[]{:S(2)}) collective-permute-start(bf16[3,2,512,512]{3,2,1,0:T(8,128)(2,1)S(1)} %pick_row.3), channel_id=1, source_target_pairs={{0,8},{8,0},{1,9},{9,1},{2,10},{10,2},{3,11},{11,3},{4,12},{12,4},... | collective-permute-start | bytes 9437192 | tf_op jit(solution)/shard_map/ppermute | solution.py:201
  7.8 4.1 %collective-permute-start.11 = (f32[2,64,512]{2,1,0:T(8,128)}, f32[2,64,512]{2,1,0:T(8,128)}, u32[]{:S(2)}, u32[]{:S(2)}) collective-permute-start(f32[2,64,512]{2,1,0:T(8,128)} %pad_maximum_fusion.1), channel_id=1, source_target_pairs={{0,8},{8,0},{1,9},{9,1},{2,10},{10,2},{3,11},{11,3},{4,12},{12,4},... | collective-permute-start | bytes 786440 | tf_op jit(solution)/shard_map/ppermute | solution.py:203
  7.8 4.0 %collective-permute-start.12 = (s32[1]{0:T(128)}, s32[1]{0:T(128)}, u32[]{:S(2)}, u32[]{:S(2)}) collective-permute-start(s32[1]{0:T(128)} %param.18), channel_id=1, source_target_pairs={{0,8},{8,0},{1,9},{9,1},{2,10},{10,2},{3,11},{11,3},{4,12},{12,4},... | collective-permute-start | bytes 20 | tf_op jit(solution)/shard_map/ppermute | solution.py:204
  11.9 10.4 %collective-permute-start.13 = (bf16[4,2,512,512]{3,2,1,0:T(8,128)(2,1)}, bf16[4,2,512,512]{3,2,1,0:T(8,128)(2,1)}, u32[]{:S(2)}, u32[]{:S(2)}) collective-permute-start(bf16[4,2,512,512]{3,2,1,0:T(8,128)(2,1)} %pick_row.2), channel_id=1, source_target_pairs={{0,8},{8,0},{1,9},{9,1},{2,10},{10,2},{3,11},{11,3},{4,12},{12,4},... | collective-permute-start | bytes 12582920 | tf_op jit(solution)/shard_map/ppermute | solution.py:208
  14.9 4.6 %collective-permute-start.7 = (bf16[64,512]{1,0:T(8,128)(2,1)S(1)}, bf16[64,512]{1,0:T(8,128)(2,1)S(1)}, u32[]{:S(2)}, u32[]{:S(2)}) collective-permute-start(bf16[64,512]{1,0:T(8,128)(2,1)S(1)} %get-tuple-element.1923.refs_0_), channel_id=1, source_target_pairs={{0,8},{8,0},{1,9},{9,1},{2,10},{10,2},{3,11},{11,3},{4,12},{12,4},... | collective-permute-start | bytes 196616 | tf_op jit(solution)/shard_map/while/body/ppermute | solution.py:229
  15.4 6.5 %collective-permute-start.6 = (bf16[64,512]{1,0:T(8,128)(2,1)S(1)}, bf16[64,512]{1,0:T(8,128)(2,1)S(1)}, u32[]{:S(2)}, u32[]{:S(2)}) collective-permute-start(bf16[64,512]{1,0:T(8,128)(2,1)S(1)} %get-tuple-element.1923.refs_0_), channel_id=1, source_target_pairs={{8,1},{1,8},{9,2},{2,9},{10,3},{3,10},{11,12},{12,11},{4,13},{13,4... | collective-permute-start | bytes 196616 | tf_op jit(solution)/shard_map/while/body/ppermute | solution.py:228
  22.4 3.6 collective-permute-start
  22.5 7.0 %collective-permute-start.2 = (bf16[64,512]{1,0:T(8,128)(2,1)S(1)}, bf16[64,512]{1,0:T(8,128)(2,1)S(1)}, u32[]{:S(2)}, u32[]{:S(2)}) collective-permute-start(bf16[64,512]{1,0:T(8,128)(2,1)S(1)} %get-tuple-element.1233), channel_id=1, source_target_pairs={{1,24},{24,1},{2,25},{25,2},{3,26},{26,3},{4,29},{29,4},{5,30},{30... | collective-permute-start | bytes 196616 | tf_op jit(solution)/shard_map/while/body/eval_jaxpr/cond/branch_1_fun/ppermute | solution.py:254
  26.0 3.5 collective-permute-start.1
  31.9 336.2 %collective-permute-start = (bf16[64,512]{1,0:T(8,128)(2,1)S(1)}, bf16[64,512]{1,0:T(8,128)(2,1)S(1)}, u32[]{:S(2)}, u32[]{:S(2)}) collective-permute-start(bf16[64,512]{1,0:T(8,128)(2,1)S(1)} %get-tuple-element.1233), channel_id=1, source_target_pairs={{0,16},{16,0},{1,17},{17,1},{2,18},{18,2},{3,19},{19,3},{4,20},{20... | collective-permute-start | bytes 196616 | tf_op jit(solution)/shard_map/while/body/eval_jaxpr/cond/branch_1_fun/ppermute | solution.py:253
  365.3 6.5 %collective-permute-start.2 = (bf16[64,512]{1,0:T(8,128)(2,1)S(1)}, bf16[64,512]{1,0:T(8,128)(2,1)S(1)}, u32[]{:S(2)}, u32[]{:S(2)}) collective-permute-start(bf16[64,512]{1,0:T(8,128)(2,1)S(1)} %get-tuple-element.1233), channel_id=1, source_target_pairs={{1,24},{24,1},{2,25},{25,2},{3,26},{26,3},{4,29},{29,4},{5,30},{30... | collective-permute-start | bytes 196616 | tf_op jit(solution)/shard_map/while/body/eval_jaxpr/cond/branch_1_fun/ppermute | solution.py:254
  368.1 3.7 collective-permute-start.1
  372.4 4.4 %collective-permute-start.9 = (bf16[64,512]{1,0:T(8,128)(2,1)S(1)}, bf16[64,512]{1,0:T(8,128)(2,1)S(1)}, u32[]{:S(2)}, u32[]{:S(2)}) collective-permute-start(bf16[64,512]{1,0:T(8,128)(2,1)S(1)} %get-tuple-element.1859.refs_0_), channel_id=1, source_target_pairs={{0,8},{8,0},{1,9},{9,1},{2,10},{10,2},{3,11},{11,3},{4,12},{12,4},... | collective-permute-start | bytes 196616 | tf_op jit(solution)/shard_map/while/body/eval_jaxpr/while/body/ppermute | solution.py:229
  372.5 6.7 %collective-permute-start.8 = (bf16[64,512]{1,0:T(8,128)(2,1)S(1)}, bf16[64,512]{1,0:T(8,128)(2,1)S(1)}, u32[]{:S(2)}, u32[]{:S(2)}) collective-permute-start(bf16[64,512]{1,0:T(8,128)(2,1)S(1)} %get-tuple-element.1859.refs_0_), channel_id=1, source_target_pairs={{8,1},{1,8},{9,2},{2,9},{10,3},{3,10},{11,12},{12,11},{4,13},{13,4... | collective-permute-start | bytes 196616 | tf_op jit(solution)/shard_map/while/body/eval_jaxpr/while/body/ppermute | solution.py:228
  379.6 4.0 %collective-permute-start.9 = (bf16[64,512]{1,0:T(8,128)(2,1)S(1)}, bf16[64,512]{1,0:T(8,128)(2,1)S(1)}, u32[]{:S(2)}, u32[]{:S(2)}) collective-permute-start(bf16[64,512]{1,0:T(8,128)(2,1)S(1)} %get-tuple-element.1859.refs_0_), channel_id=1, source_target_pairs={{0,8},{8,0},{1,9},{9,1},{2,10},{10,2},{3,11},{11,3},{4,12},{12,4},... | collective-permute-start | bytes 196616 | tf_op jit(solution)/shard_map/while/body/eval_jaxpr/while/body/ppermute | solution.py:229
  379.7 6.4 %collective-permute-start.8 = (bf16[64,512]{1,0:T(8,128)(2,1)S(1)}, bf16[64,512]{1,0:T(8,128)(2,1)S(1)}, u32[]{:S(2)}, u32[]{:S(2)}) collective-permute-start(bf16[64,512]{1,0:T(8,128)(2,1)S(1)} %get-tuple-element.1859.refs_0_), channel_id=1, source_target_pairs={{8,1},{1,8},{9,2},{2,9},{10,3},{3,10},{11,12},{12,11},{4,13},{13,4... | collective-permute-start | bytes 196616 | tf_op jit(solution)/shard_map/while/body/eval_jaxpr/while/body/ppermute | solution.py:228
  386.4 1.4 collective-permute-start.14
